TPU v7x, 512 devices: a whole 4x8x8 slice. The times are simulated.
512 devices in a mesh: pts: 64 (over y, x, core), tm: 8 (over z).
Axes of the slice: x: 4, y: 8, z: 8, core: 2. Of those that a mesh axis runs over, the one named last changes fastest.
Arguments:
- starting_location_factors: float32 [32768, 128], P('pts'), may hold values from -5 to 5
- starting_temporal_factors: float32 [8192, 128], P('tm'), may hold values from -5 to 5
- imposed_tension_record: float32 [32768, 8192], P('pts', 'tm'), may hold values from -10 to 10
- viscous_rate_factor: float32 [32768], P('pts'), may hold values from 0.2 to 1
- norton_power_law: float32 [32768], P('pts'), may hold values from 1.2 to 2.2
- space_inverse: float32 [128, 128], replicated, may hold values from -2 to 2
- time_inverse: float32 [128, 128], replicated, may hold values from -2 to 2
Outputs:
- space_out: float32 [32768, 128], P('pts')
- time_out: float32 [8192, 128], P('tm')
- misfit: float32 [2], replicated
All inputs are finite; a program needn't handle non-finite values.
Results may differ from a plain program's by a relative error of at most 0.0005.
Values sent between devices are 32-bit elements; how exact they have to be, the bound alone decides.
A program may use at most 64 MiB of HBM per device.

v0:
```python
import math

import jax
import jax.numpy as jnp
from jax import lax
from jax.sharding import PartitionSpec as P

ITERS = 2


highest = lax.Precision.HIGHEST


def viscous_pass(
    starting_location_factors,
    starting_temporal_factors,
    imposed_tension_record,
    viscous_rate_factor,
    norton_power_law,
):
    rank_scale = 1.0 / math.sqrt(starting_location_factors.shape[1])
    recon_field = (
        jnp.dot(starting_location_factors, starting_temporal_factors.T, precision=highest)
        * rank_scale
    )
    stress = imposed_tension_record - recon_field
    flow_rate = (
        viscous_rate_factor[:, None]
        * stress
        * jnp.power(stress * stress + 1e-06, 0.5 * (norton_power_law[:, None] - 1.0))
    )
    return (stress, flow_rate)


def shards(
    starting_location_factors,
    starting_temporal_factors,
    imposed_tension_record,
    viscous_rate_factor,
    norton_power_law,
    space_inverse,
    time_inverse,
):
    pts_count = lax.axis_size("pts")
    instant_count = lax.axis_size("tm")
    point_total = starting_location_factors.shape[0] * pts_count
    instant_total = starting_temporal_factors.shape[0] * instant_count
    share_rows = starting_temporal_factors.shape[0] // pts_count
    residual_record = []
    for sweep in range(ITERS):
        stress, flow_rate = viscous_pass(
            starting_location_factors,
            starting_temporal_factors,
            imposed_tension_record,
            viscous_rate_factor,
            norton_power_law,
        )
        residual_energy = jnp.sum(stress * stress)
        time_part = lax.dot_general(
            flow_rate, starting_location_factors, (((0,), (0,)), ((), ())), precision=highest
        )
        time_sum = lax.psum(time_part, "pts")
        temporal_factors_before_rescale = jnp.dot(time_sum, time_inverse, precision=highest)
        own_start = lax.axis_index("pts") * share_rows
        own_block = lax.dynamic_slice_in_dim(
            temporal_factors_before_rescale, own_start, share_rows, 0
        )
        temporal_magnitude_quad = jnp.sum(own_block * own_block, axis=0)
        space_part = jnp.dot(flow_rate, starting_temporal_factors, precision=highest)
        space_sum = lax.psum(space_part, "tm")
        space_raw = jnp.dot(space_sum, space_inverse, precision=highest)
        space_sq = jnp.sum(space_raw * space_raw, axis=0)
        space_sq = lax.psum(space_sq, "pts")
        temporal_magnitude_quad = lax.psum(temporal_magnitude_quad, ("pts", "tm"))
        residual_energy = lax.psum(residual_energy, ("pts", "tm"))
        starting_location_factors = space_raw / jnp.sqrt(space_sq / point_total + 1e-06)
        updated_time_modes = temporal_factors_before_rescale / jnp.sqrt(
            temporal_magnitude_quad / instant_total + 1e-06
        )
        starting_temporal_factors = updated_time_modes
        residual_record.append(residual_energy / (point_total * instant_total))
    return (starting_location_factors, starting_temporal_factors, jnp.stack(residual_record))


def solution(mesh):
    return jax.shard_map(
        shards,
        mesh=mesh,
        in_specs=(P("pts", None), P("tm", None), P("pts", "tm"), P("pts"), P("pts"), P(), P()),
        out_specs=(P("pts", None), P("tm", None), P()),
        check_vma=False,
    )
```

profile of v0, /device:TPU:1, one launch (start us, length us, event | category | flops | bytes accessed | tf_op | source)
XLA Modules:
  0.0 881.4 jit_solution(14366667147604201860)
XLA Ops:
  7.2 0.0 all-reduce.8.cloned.1.call-start
  7.2 0.7 add_multiply_fusion
  8.0 0.3 copy-done
  8.2 4.5 multiply_reduce_fusion.1
  12.7 1.3 copy-done.3
  14.1 7.1 fusion
  21.2 0.0 all-reduce.8.cloned.1.call-update
  21.3 0.2 all-reduce.6.cloned.1.call-start
  21.5 7.3 fusion.1
  28.8 0.0 all-reduce.6.cloned.1.call-update
  28.8 0.0 all-reduce.12.cloned.1.call-start
  28.9 189.0 %all-reduce.8.cloned.1.call-done = f32[1024,128]{1,0:T(8,128)} async-done(((f32[1024,128]{1,0:T(8,128)}), f32[1024,128]{1,0:T(8,128)}) %all-reduce.8.cloned.1.call-update) | async-done | bytes 524304 | tf_op jit(solution)/shard_map/psum | solution.py:62
  217.9 1.6 fusion.20
  219.5 99.1 %psum.73 = f32[128]{0:T(128)S(1)} all-reduce(f32[128]{0:T(128)S(1)} %multiply_reduce_fusion.5), channel_id=1, replica_groups=mesh['pts'=64,'tm'=8] {'pts','tm'}, use_global_device_ids=true, to_apply=%region_5.0 | all-reduce | flops 128 | bytes 1024 | tf_op jit(solution)/shard_map/psum | solution.py:74
  318.6 1.3 multiply_reduce_fusion.3
  319.9 125.1 %psum.71 = f32[128]{0:T(128)} all-reduce(f32[128]{0:T(128)S(1)} %get-tuple-element.6), channel_id=1, replica_groups=mesh['pts'=64,'tm'=8] {'pts'}, use_global_device_ids=true, to_apply=%region_2.0 | all-reduce | flops 128 | bytes 1024 | tf_op jit(solution)/shard_map/psum | solution.py:73
  445.0 0.7 add_sqrt_fusion.3
  445.7 2.8 multiply_reduce_fusion
  448.5 1.3 copy-done.2
  449.9 7.1 fusion.2
  457.0 0.0 all-reduce.12.cloned.1.call-update
  457.0 0.3 all-reduce.10.cloned.1.call-start
  457.3 7.3 fusion.3
  464.6 0.0 all-reduce.10.cloned.1.call-update
  464.6 180.4 %all-reduce.12.cloned.1.call-done = f32[1024,128]{1,0:T(8,128)} async-done(((f32[1024,128]{1,0:T(8,128)}), f32[1024,128]{1,0:T(8,128)}) %all-reduce.12.cloned.1.call-update) | async-done | bytes 524304 | tf_op jit(solution)/shard_map/psum | solution.py:62
  645.0 1.6 fusion.21
  646.6 99.2 %all-reduce = (f32[128]{0:T(128)S(1)}, f32[]{:T(128)}, f32[]{:T(128)}) all-reduce(f32[128]{0:T(128)S(1)} %multiply_reduce_fusion.4, f32[]{:T(128)} %get-tuple-element.10, f32[]{:T(128)} %get-tuple-element.12), channel_id=1, replica_groups=mesh['pts'=64,'tm'=8] {'pts','tm'}, use_global_device_ids=true, to_apply=%region_11.0 | all-reduce | flops 130 | bytes 1040 | tf_op jit(solution)/shard_map/psum | solution.py:74
  747.1 0.8 broadcast_divide_fusion
  748.0 1.3 multiply_reduce_fusion.2
  749.3 124.2 %psum.75 = f32[128]{0:T(128)S(1)} all-reduce(f32[128]{0:T(128)S(1)} %get-tuple-element.8), channel_id=1, replica_groups=mesh['pts'=64,'tm'=8] {'pts'}, use_global_device_ids=true, to_apply=%region_8.0 | all-reduce | flops 128 | bytes 1024 | tf_op jit(solution)/shard_map/psum | solution.py:73
  873.5 0.6 pad_maximum_fusion
  874.1 0.7 broadcast_divide_fusion.4
  (20 shorter events, 0.1 us)
Async XLA Ops:
  7.2 1.1 copy-start
  7.2 210.7 %all-reduce.8.cloned.1.call-start = ((), (), s32[]{:S(2)}) async-start(), calls=%async_computation.1 | async-start | bytes 1048576 | tf_op jit(solution)/shard_map/psum | solution.py:62
  8.2 5.9 copy-start.4
  8.2 5.9 copy-start.7
  12.7 1.4 copy-start.3
  21.2 196.7 %copy-start.5 = (f32[128,128]{1,0:T(8,128)S(1)}, f32[128,128]{1,0:T(8,128)}, u32[]{:S(2)}) copy-start(f32[128,128]{1,0:T(8,128)} %param.13) | copy-start | bytes 196612
  21.2 297.4 %copy-start.6 = (f32[128,128]{1,0:T(8,128)S(1)}, f32[128,128]{1,0:T(8,128)}, u32[]{:S(2)}) copy-start(f32[128,128]{1,0:T(8,128)} %param.12) | copy-start | bytes 196612
  21.3 424.4 %copy-start.1 = (f32[512,1024]{1,0:T(8,128)S(1)}, f32[512,1024]{1,0:T(8,128)}, u32[]{:S(2)}) copy-start(f32[512,1024]{1,0:T(8,128)} %param.9) | copy-start | bytes 6291460
  21.3 297.3 %all-reduce.6.cloned.1.call-start = ((), (), s32[]{:S(2)}) async-start(), calls=%async_computation | async-start | bytes 524288 | tf_op jit(solution)/shard_map/psum | solution.py:70
  28.8 616.1 %all-reduce.12.cloned.1.call-start = ((), (), s32[]{:S(2)}) async-start(), calls=%async_computation.3 | async-start | bytes 1048576 | tf_op jit(solution)/shard_map/psum | solution.py:62
  448.5 1.4 copy-start.2
  457.0 290.9 %all-reduce.10.cloned.1.call-start = ((), (), s32[]{:S(2)}) async-start(), calls=%async_computation.2 | async-start | bytes 524288 | tf_op jit(solution)/shard_map/psum | solution.py:70
Sparse Core Ops, SparseCore 0:
  21.4 196.4 all-reduce.7
  220.8 73.5 all-reduce.5
  457.1 187.8 all-reduce.11
  647.8 73.5 all-reduce.9
where the time goes:
time: 882 us; the launch traced here: 881 us
  blocking collectives  448 us (51%)
  waiting for transfers between devices  369 us (42%)
  matrix products  42 us (5%)
  between operations  15.1 us (2%)
    psum x2, waiting for transfers between devices, shards(): time_sum = lax.psum(time_part, 'pts')  369 us
    psum x2, blocking collectives, shards(): space_sq = lax.psum(space_sq, 'pts')  249 us
    psum x2, blocking collectives, shards(): temporal_magnitude_quad = lax.psum(temporal_magnitude_quad, ('pts', 'tm'))  198 us
  transfers between devices with their start and end apart: 4, of which 2 were waited for; matrix products, arithmetic and copies ran while one was open for 2% of the time, Pallas kernels for 0%

commit v1 on v0

v1 whole, which is shorter than its diff:
```python
import functools
import math

import jax
import jax.numpy as jnp
from jax import lax
from jax.experimental import pallas as pl
from jax.experimental.pallas import tpu as pltpu
from jax.sharding import PartitionSpec as P

ITERS = 2
F32, BF16 = jnp.float32, jnp.bfloat16
MESH = pl.DeviceIdType.MESH
NX, NY, NC = 4, 8, 2


def split(value):
    hi = value.astype(BF16)
    return hi, (value - hi.astype(F32)).astype(BF16)


def dot(a, b, ca, cb):
    return lax.dot_general(a, b, (((ca,), (cb,)), ((), ())), preferred_element_type=F32)


def fold(pair):
    return pair[:, :128] + pair[:, 128:]


def kernel(nz, s0, u0, sig, rate, power, inv_s, inv_t, s_out, u_out, mis_out,
           lr, ex, a_ref, b_ref, bb_ref, rec, fh, fl, tp, cr, th, xr, ts, yr, u_nx, sp, zr, s_nx, nv,
           send, recv):
    points, rank = s0.shape
    moments = u0.shape[0]
    half = moments // NC
    xrows = half // NX
    yrows = xrows // NY
    zrows = points // nz
    point_total = points * NX * NY * NC
    moment_total = moments * nz
    p, z = lax.axis_index("pts"), lax.axis_index("tm")
    c, x, y = p % NC, (p // NC) % NX, p // (NC * NX)

    def at(cc, xx, yy):
        return (yy * NX + xx) * NC + cc

    cx_peers = []
    for dc in range(NC):
        for dx in range(NX):
            if dc or dx:
                cx_peers.append(((c + dc) % NC, (x + dx) % NX))
    y_peers = [(y + d) % NY for d in range(1, NY)]
    z_peers = [(z + d) % nz for d in range(1, nz)]

    barrier = pltpu.get_barrier_semaphore()
    for cc, xx in cx_peers:
        pl.semaphore_signal(barrier, inc=1, device_id=(at(cc, xx, y), z), device_id_type=MESH)
    for yy in y_peers:
        pl.semaphore_signal(barrier, inc=1, device_id=(at(c, x, yy), z), device_id_type=MESH)
    for zz in z_peers:
        pl.semaphore_signal(barrier, inc=1, device_id=(p, zz), device_id_type=MESH)

    def put(src, dst, it, stage, pp, zz):
        pltpu.make_async_remote_copy(
            src_ref=src, dst_ref=dst, send_sem=send.at[it, stage], recv_sem=recv.at[it, stage],
            device_id=(pp, zz), device_id_type=MESH,
        ).start()

    def drain(ref, sem):
        pltpu.make_async_copy(ref, ref, sem).wait()

    for k in range(points // 128):
        rows = pl.ds(k * 128, 128)
        lr[rows, :] = jnp.broadcast_to(jnp.log2(rate[k : k + 1, :]), (128, 128)).T
        ex[rows, :] = jnp.broadcast_to(0.5 * (power[k : k + 1, :] - 1.0), (128, 128)).T

    scale_s = scale_u = None
    for it in range(ITERS):
        s_cur = s0 if it == 0 else s_nx.at[it - 1]
        u_cur = u0 if it == 0 else u_nx.at[it - 1]
        root = 1.0 / math.sqrt(rank)
        sv = s_cur[...] * (root if it == 0 else scale_s * scale_u * root)
        hi, lo = split(sv)
        a_ref[:, :128] = hi
        a_ref[:, 128:] = lo
        hi, lo = split(u_cur[...])
        b_ref[:, :128] = hi
        b_ref[:, 128:] = lo
        bb_ref[...] = hi

        def flow_block(j, mis):
            cols = pl.ds(pl.multiple_of(j * 256, 256), 256)
            ub = b_ref[cols, :]
            rec[...] = dot(a_ref[:, :128], ub[:, :128], 1, 1) + dot(a_ref[:, :128], ub[:, 128:], 1, 1) + dot(
                a_ref[:, 128:], ub[:, :128], 1, 1)
            for r in range(points // 64):
                rows = pl.ds(r * 64, 64)
                for h in range(2):
                    lanes = pl.ds(h * 128, 128)
                    cl = pl.ds(pl.multiple_of(j * 256 + h * 128, 128), 128)
                    stress = sig[rows, cl] - rec[rows, lanes]
                    quad = stress * stress
                    mis = mis + jnp.sum(quad.reshape(8, 8, 128), axis=0)
                    flow = stress * jnp.exp2(lr[rows, :] + ex[rows, :] * jnp.log2(quad + 1e-6))
                    hi, lo = split(flow)
                    fh[rows, cl] = hi
                    fl[rows, cl] = lo
            return mis

        mis = lax.fori_loop(0, moments // 256, flow_block, jnp.zeros((8, 128), F32))

        if it == 0:
            pl.semaphore_wait(barrier, len(cx_peers) + len(y_peers) + len(z_peers))

        def time_half(cc):
            cols = pl.ds(pl.multiple_of(cc * half, half), half)
            tp[it, cols, :] = fold(dot(fh[:, cols], a_ref[...], 0, 0) + dot(fl[:, cols], a_ref[...], 0, 0))
            return cols

        cols = time_half(1 - c)
        put(tp.at[it, cols, :], cr.at[it], it, 0, at(1 - c, x, y), z)
        cols = time_half(c)
        sp[it] = fold(dot(fh[...], b_ref[...], 1, 0) + dot(fl[...], b_ref[...], 1, 0))
        for d, zz in enumerate(z_peers):
            rows = pl.ds(pl.multiple_of(zz * zrows, zrows), zrows)
            put(sp.at[it, rows, :], zr.at[it, d], it, 1, p, zz)
        drain(cr.at[it], recv.at[it, 0])
        th[it] = tp[it, cols, :] + cr[it]
        for d in range(1, NX):
            xx = (x + d) % NX
            rows = pl.ds(pl.multiple_of(xx * xrows, xrows), xrows)
            put(th.at[it, rows, :], xr.at[it, d - 1], it, 2, at(c, xx, y), z)
        drain(xr.at[it], recv.at[it, 2])
        rows = pl.ds(pl.multiple_of(x * xrows, xrows), xrows)
        ts[it] = th[it, rows, :] + xr[it, 0] + xr[it, 1] + xr[it, 2]
        for d, yy in enumerate(y_peers):
            rows = pl.ds(pl.multiple_of(yy * yrows, yrows), yrows)
            put(ts.at[it, rows, :], yr.at[it, d], it, 3, at(c, x, yy), z)
        drain(zr.at[it], recv.at[it, 1])
        own_z = pl.ds(pl.multiple_of(z * zrows, zrows), zrows)
        piece = sp[it, own_z, :]
        for d in range(nz - 1):
            piece = piece + zr[it, d]
        if it > 0:
            piece = piece * scale_u
        s_raw = jnp.dot(piece, inv_s[...], precision=lax.Precision.HIGHEST, preferred_element_type=F32)
        s_nx[it, own_z, :] = s_raw
        for zz in z_peers:
            put(s_nx.at[it, own_z, :], s_nx.at[it, own_z, :], it, 4, p, zz)
        s_sq = jnp.sum(s_raw * s_raw, axis=0, keepdims=True)

        drain(yr.at[it], recv.at[it, 3])
        rows = pl.ds(pl.multiple_of(y * yrows, yrows), yrows)
        piece = ts[it, rows, :]
        for d in range(NY - 1):
            piece = piece + yr[it, d]
        piece = piece * (math.sqrt(rank) if it == 0 else math.sqrt(rank) / scale_u)
        t_raw = jnp.dot(piece, inv_t[...], precision=lax.Precision.HIGHEST, preferred_element_type=F32)
        own_t = pl.ds(pl.multiple_of(c * half + x * xrows + y * yrows, yrows), yrows)
        u_nx[it, own_t, :] = t_raw
        for yy in y_peers:
            put(u_nx.at[it, own_t, :], u_nx.at[it, own_t, :], it, 5, at(c, x, yy), z)
        t_sq = jnp.sum(t_raw * t_raw, axis=0, keepdims=True)

        mis = jnp.sum(mis, axis=0, keepdims=True)
        row = lax.broadcasted_iota(jnp.int32, (8, 128), 0)
        vec = jnp.where(row == 0, s_sq, jnp.where(row == 1, t_sq, jnp.where(row == 2, mis, 0.0)))
        me = c * NX + x
        nv[it, 0, me] = vec
        for cc, xx in cx_peers:
            put(nv.at[it, 0, me], nv.at[it, 0, me], it, 6, at(cc, xx, y), z)

        drain(yr.at[it], recv.at[it, 5])
        own_x = pl.ds(pl.multiple_of(c * half + x * xrows, xrows), xrows)
        for d in range(1, NX):
            put(u_nx.at[it, own_x, :], u_nx.at[it, own_x, :], it, 7, at(c, (x + d) % NX, y), z)

        drain(nv.at[it, 0, pl.ds(0, 7)], recv.at[it, 6])
        vec = nv[it, 0, 0]
        for k in range(1, 8):
            vec = vec + nv[it, 0, k]
        nv[it, 1, y] = vec
        for yy in y_peers:
            put(nv.at[it, 1, y], nv.at[it, 1, y], it, 8, at(c, x, yy), z)

        drain(xr.at[it], recv.at[it, 7])
        own_c = pl.ds(pl.multiple_of(c * half, half), half)
        put(u_nx.at[it, own_c, :], u_nx.at[it, own_c, :], it, 9, at(1 - c, x, y), z)

        drain(nv.at[it, 1, pl.ds(0, 7)], recv.at[it, 8])
        vec = nv[it, 1, 0]
        for k in range(1, 8):
            vec = vec + nv[it, 1, k]
        nv[it, 2, z] = vec
        for zz in z_peers:
            put(nv.at[it, 2, z], nv.at[it, 2, z], it, 10, p, zz)
        drain(cr.at[it], recv.at[it, 9])
        drain(zr.at[it], recv.at[it, 4])
        drain(nv.at[it, 2, pl.ds(0, 7)], recv.at[it, 10])
        vec = nv[it, 2, 0]
        for k in range(1, 8):
            vec = vec + nv[it, 2, k]
        scale_s = 1.0 / jnp.sqrt(vec[0:1, :] / point_total + 1e-6)
        scale_u = 1.0 / jnp.sqrt(vec[1:2, :] / moment_total + 1e-6)
        mis_out[it] = jnp.sum(vec[2:3, :]) / (point_total * moment_total)

    s_out[...] = s_nx[ITERS - 1] * scale_s
    u_out[...] = u_nx[ITERS - 1] * scale_u
    for it in range(ITERS):
        for stage, ref in enumerate((cr, zr, xr, yr, zr, yr, None, xr, None, cr, None)):
            drain(nv.at[it, 0, pl.ds(0, 7)] if ref is None else ref.at[it], send.at[it, stage])


def shards(nz, s0, u0, sig, rate, power, inv_s, inv_t):
    points, rank = s0.shape
    moments = u0.shape[0]
    half = moments // NC
    xrows = half // NX
    yrows = xrows // NY
    zrows = points // nz
    vmem = pl.BlockSpec(memory_space=pltpu.VMEM)
    return pl.pallas_call(
        functools.partial(kernel, nz),
        out_shape=(
            jax.ShapeDtypeStruct((points, rank), F32),
            jax.ShapeDtypeStruct((moments, rank), F32),
            jax.ShapeDtypeStruct((ITERS,), F32),
        ),
        in_specs=[vmem] * 7,
        out_specs=(vmem, vmem, pl.BlockSpec(memory_space=pltpu.SMEM)),
        scratch_shapes=[
            pltpu.VMEM((points, 128), F32),
            pltpu.VMEM((points, 128), F32),
            pltpu.VMEM((points, 2 * rank), BF16),
            pltpu.VMEM((moments, 2 * rank), BF16),
            pltpu.VMEM((moments, rank), BF16),
            pltpu.VMEM((points, 256), F32),
            pltpu.VMEM((points, moments), BF16),
            pltpu.VMEM((points, moments), BF16),
            pltpu.VMEM((ITERS, moments, rank), F32),
            pltpu.VMEM((ITERS, half, rank), F32),
            pltpu.VMEM((ITERS, half, rank), F32),
            pltpu.VMEM((ITERS, NX - 1, xrows, rank), F32),
            pltpu.VMEM((ITERS, xrows, rank), F32),
            pltpu.VMEM((ITERS, NY - 1, yrows, rank), F32),
            pltpu.VMEM((ITERS, moments, rank), F32),
            pltpu.VMEM((ITERS, points, rank), F32),
            pltpu.VMEM((ITERS, nz - 1, zrows, rank), F32),
            pltpu.VMEM((ITERS, points, rank), F32),
            pltpu.VMEM((ITERS, 3, 8, 8, 128), F32),
            pltpu.SemaphoreType.DMA((ITERS, 11)),
            pltpu.SemaphoreType.DMA((ITERS, 11)),
        ],
        compiler_params=pltpu.CompilerParams(
            collective_id=0, has_side_effects=True, vmem_limit_bytes=40 * 1024 * 1024
        ),
    )(s0, u0, sig, rate.reshape(points // 128, 128), power.reshape(points // 128, 128), inv_s, inv_t)


def solution(mesh):
    return jax.shard_map(
        functools.partial(shards, mesh.shape["tm"]),
        mesh=mesh,
        in_specs=(P("pts", None), P("tm", None), P("pts", "tm"), P("pts"), P("pts"), P(), P()),
        out_specs=(P("pts", None), P("tm", None), P()),
        check_vma=False,
    )
```

time: 882 us -> 82 us (0.09)
  blocking collectives: 448 us -> 0 us
  waiting for transfers between devices: 369 us -> 0 us
  Pallas kernels: 0 us -> 71.1 us
  matrix products: 42 us -> 0 us
  between operations: 15.1 us -> 0.66 us
    psum x4 -> x0, blocking collectives: 448 us -> none  [the longest x2 249 us: shards(): space_sq = lax.psum(space_sq, 'pts')]
    psum x4 -> x0, waiting for transfers between devices: 369 us -> none  [the longest x2 369 us: shards(): time_sum = lax.psum(time_part, 'pts')]
    pallas_call x0 -> x1, Pallas kernels: none -> 71.1 us  [shards(): pl.pallas_call(functools.partial(kernel, nz), out_shape=(jax.ShapeDtypeSt...]
    dot_general x10 -> x0, matrix products: 42 us -> none  [the longest x2 14.6 us: shards(): jnp.dot(flow_rate, starting_temporal_factors, precision=highest)]
  transfers between devices with their start and end apart: 4 -> 0, of which waited for: 2 -> 0; matrix products, arithmetic and copies ran while one was open for 2% -> 0% of each run, Pallas kernels for 0% -> 0%
where the time goes in v1:
time: 82 us; the launch traced here: 80.4 us
  Pallas kernels  71.1 us (87%)
  local copies, waits for them, and re-layouts  8.62 us (11%)
    pallas_call x1, Pallas kernels, shards(): pl.pallas_call(functools.partial(kernel, nz), out_shape=(jax.ShapeDtypeSt...  71.1 us
    unnamed x17, local copies, waits for them, and re-layouts  8.62 us

profile of v1, /device:TPU:1, one launch (start us, length us, event | category | flops | bytes accessed | tf_op | source)
XLA Modules:
  0.0 80.4 jit_solution(17037278913622098716)
XLA Ops:
  0.6 0.0 copy-start
  0.6 1.6 %copy-done = f32[512,1024]{1,0:T(8,128)S(1)} copy-done((f32[512,1024]{1,0:T(8,128)S(1)}, f32[512,1024]{1,0:T(8,128)}, u32[]{:S(2)}) %copy-start) | copy-done | bytes 2097176
  2.2 0.0 copy-start.1
  2.2 1.0 %copy-done.1 = f32[1024,128]{1,0:T(8,128)S(1)} copy-done((f32[1024,128]{1,0:T(8,128)S(1)}, f32[1024,128]{1,0:T(8,128)}, u32[]{:S(2)}) %copy-start.1) | copy-done | bytes 524312
  3.3 0.0 copy-start.2
  3.3 0.9 %copy-done.2 = f32[512,128]{1,0:T(8,128)S(1)} copy-done((f32[512,128]{1,0:T(8,128)S(1)}, f32[512,128]{1,0:T(8,128)}, u32[]{:S(2)}) %copy-start.2) | copy-done | bytes 262168
  4.2 0.0 copy-start.3
  4.2 0.8 %copy-done.3 = f32[128,128]{1,0:T(8,128)S(1)} copy-done((f32[128,128]{1,0:T(8,128)S(1)}, f32[128,128]{1,0:T(8,128)}, u32[]{:S(2)}) %copy-start.3) | copy-done | bytes 65560
  5.1 0.0 copy-start.4
  5.1 0.8 %copy-done.4 = f32[128,128]{1,0:T(8,128)S(1)} copy-done((f32[128,128]{1,0:T(8,128)S(1)}, f32[128,128]{1,0:T(8,128)}, u32[]{:S(2)}) %copy-start.4) | copy-done | bytes 65560
  5.9 0.0 copy-start.5
  5.9 0.7 copy-done.5
  6.6 0.0 copy-start.6
  6.6 0.7 copy-done.6
  7.3 71.1 %shard_map.94 = (f32[512,128]{1,0:T(8,128)S(1)}, f32[1024,128]{1,0:T(8,128)S(1)}, f32[2]{0:T(128)S(1)}) custom-call(f32[512,128]{1,0:T(8,128)S(1)} %copy-done.2, f32[1024,128]{1,0:T(8,128)S(1)} %copy-done.1, f32[512,1024]{1,0:T(8,128)S(1)} %copy-done, f32[4,128]{1,0:T(4,128)S(1)} %bitcast.2, f32[4,128]{1,0:T(4,128)S(1)} %bitcast.3, ...), custom_call_target="tpu_custom_call" | custom-call | tf_op jit(solution)/shard_map/pallas_call | solution.py:222
  78.4 0.7 copy.13
  79.1 0.8 copy.14
  79.9 0.5 copy.15
Async XLA Ops:
  0.6 1.6 %copy-start = (f32[512,1024]{1,0:T(8,128)S(1)}, f32[512,1024]{1,0:T(8,128)}, u32[]{:S(2)}) copy-start(f32[512,1024]{1,0:T(8,128)} %sig.1) | copy-start | bytes 6291460
  2.2 1.0 %copy-start.1 = (f32[1024,128]{1,0:T(8,128)S(1)}, f32[1024,128]{1,0:T(8,128)}, u32[]{:S(2)}) copy-start(f32[1024,128]{1,0:T(8,128)} %u0.1) | copy-start | bytes 1572868
  3.3 0.9 %copy-start.2 = (f32[512,128]{1,0:T(8,128)S(1)}, f32[512,128]{1,0:T(8,128)}, u32[]{:S(2)}) copy-start(f32[512,128]{1,0:T(8,128)} %s0.1) | copy-start | bytes 786436
  4.2 0.8 %copy-start.3 = (f32[128,128]{1,0:T(8,128)S(1)}, f32[128,128]{1,0:T(8,128)}, u32[]{:S(2)}) copy-start(f32[128,128]{1,0:T(8,128)} %inv_s.1) | copy-start | bytes 196612
  5.1 0.8 %copy-start.4 = (f32[128,128]{1,0:T(8,128)S(1)}, f32[128,128]{1,0:T(8,128)}, u32[]{:S(2)}) copy-start(f32[128,128]{1,0:T(8,128)} %inv_t.1) | copy-start | bytes 196612
  5.9 0.7 copy-start.5
  6.6 0.7 copy-start.6

commit v2 on v1

v2 whole, which is shorter than its diff:
```python
import functools
import math

import jax
import jax.numpy as jnp
from jax import lax
from jax.experimental import pallas as pl
from jax.experimental.pallas import tpu as pltpu
from jax.sharding import PartitionSpec as P

ITERS = 2
F32, BF16 = jnp.float32, jnp.bfloat16
MESH = pl.DeviceIdType.MESH
NX, NY, NC = 4, 8, 2
ORDER = (2, 1, 3, 0)
X_SUM, Y_SUM, Z_SUM, Z_ALL, Y_ALL, X_ALL, C_ALL, N_CX, N_Y, N_Z, STAGES = range(2, 13)


def split(value):
    hi = value.astype(BF16)
    return hi, (value - hi.astype(F32)).astype(BF16)


def dot(a, b, ca, cb):
    return lax.dot_general(a, b, (((ca,), (cb,)), ((), ())), preferred_element_type=F32)


def kernel(nz, s_in, u_in, sig_in, rate_in, power_in, inv_s_in, inv_t_in, s_out, u_out, mis_out,
           s0, u0, sig, rate, power, inv_s, inv_t,
           lr, ex, a_ref, at_ref, b_ref, rec, fh, fl, tp, cr, th, xr, ts, yr, u_nx, sp, zr, s_nx, nv,
           load, send, recv):
    points, rank = s0.shape
    moments = u0.shape[0]
    half = moments // NC
    xrows = half // NX
    yrows = xrows // NY
    zrows = points // nz
    blocks = moments // xrows
    point_total = points * NX * NY * NC
    moment_total = moments * nz
    p, z = lax.axis_index("pts"), lax.axis_index("tm")
    c, x, y = p % NC, (p // NC) % NX, p // (NC * NX)

    def at(cc, xx, yy):
        return (yy * NX + xx) * NC + cc

    cx_peers = []
    for dc in range(NC):
        for dx in range(NX):
            if dc or dx:
                cx_peers.append(((c + dc) % NC, (x + dx) % NX))
    y_peers = [(y + d) % NY for d in range(1, NY)]
    z_peers = [(z + d) % nz for d in range(1, nz)]

    starts = []
    for side in (1 - c, c):
        for d in ORDER:
            starts.append(pl.multiple_of(side * half + (x + d) % NX * xrows, xrows))

    loads = []

    def fetch(src, dst):
        cp = pltpu.make_async_copy(src, dst, load.at[len(loads)])
        cp.start()
        loads.append(cp)
        return cp

    u_load, s_load = fetch(u_in, u0), fetch(s_in, s0)
    rate_load, power_load = fetch(rate_in, rate), fetch(power_in, power)
    sig_load = [fetch(sig_in.at[:, pl.ds(q, xrows)], sig.at[k]) for k, q in enumerate(starts)]
    inv_loads = [fetch(inv_s_in, inv_s), fetch(inv_t_in, inv_t)]

    barrier = pltpu.get_barrier_semaphore()
    for cc, xx in cx_peers:
        pl.semaphore_signal(barrier, inc=1, device_id=(at(cc, xx, y), z), device_id_type=MESH)
    for yy in y_peers:
        pl.semaphore_signal(barrier, inc=1, device_id=(at(c, x, yy), z), device_id_type=MESH)
    for zz in z_peers:
        pl.semaphore_signal(barrier, inc=1, device_id=(p, zz), device_id_type=MESH)

    def put(src, dst, it, stage, pp, zz):
        pltpu.make_async_remote_copy(
            src_ref=src, dst_ref=dst, send_sem=send.at[it, stage], recv_sem=recv.at[it, stage],
            device_id=(pp, zz), device_id_type=MESH,
        ).start()

    def drain(ref, sem, it, stage):
        pltpu.make_async_copy(ref, ref, sem.at[it, stage]).wait()

    def split_time(u_cur):
        for k, q in enumerate(starts):
            rows = pl.ds(k * xrows, xrows)
            hi, lo = split(u_cur[pl.ds(q, xrows), :])
            b_ref[rows, :rank] = hi
            b_ref[rows, rank : 2 * rank] = hi
            b_ref[rows, 2 * rank : 3 * rank] = lo
            b_ref[rows, 3 * rank :] = lo

    rate_load.wait()
    power_load.wait()
    for k in range(points // 128):
        rows = pl.ds(k * 128, 128)
        lr[rows, :] = jnp.broadcast_to(jnp.log2(rate[k : k + 1, :]), (128, 128)).T
        ex[rows, :] = jnp.broadcast_to(0.5 * (power[k : k + 1, :] - 1.0), (128, 128)).T
    u_load.wait()
    split_time(u0)
    s_load.wait()

    scale_s = scale_u = None
    for it in range(ITERS):
        s_cur = s0 if it == 0 else s_nx.at[it - 1]
        root = 1.0 / math.sqrt(rank)
        factor = root if it == 0 else scale_s * scale_u * root
        for k in range(points // 128):
            rows = pl.ds(k * 128, 128)
            sv = s_cur[rows, :] * factor
            hi, lo = split(sv)
            a_ref[rows, :rank] = hi
            a_ref[rows, rank:] = lo
            hi, lo = split(sv.T)
            at_ref[:rank, rows] = hi
            at_ref[rank:, rows] = lo

        def rebuild(m):
            rows = pl.ds(2 * m * xrows, 2 * xrows)
            rec[m % 2] = dot(a_ref[...], b_ref[rows, : 2 * rank], 1, 1) + dot(a_ref[...], b_ref[rows, 2 * rank :], 1, 1)

        def respond(m, mis):
            for k in (2 * m, 2 * m + 1):
                lanes = pl.ds(k * xrows, xrows)
                for r in range(points // 64):
                    rows = pl.ds(r * 64, 64)
                    stress = sig[k, rows, :] - rec[m % 2, rows, pl.ds((k % 2) * xrows, xrows)]
                    quad = stress * stress
                    mis = mis + jnp.sum(quad.reshape(8, 8, 128), axis=0)
                    flow = stress * jnp.exp2(lr[rows, :] + ex[rows, :] * jnp.log2(quad + 1e-6))
                    hi, lo = split(flow)
                    fh[rows, lanes] = hi
                    fl[rows, lanes] = lo
            return mis

        def time_part(m):
            lanes = pl.ds(2 * m * xrows, 2 * xrows)
            pair = dot(at_ref[...], fh[:, lanes], 1, 0)
            part = pair[:rank] + pair[rank:] + dot(at_ref[:rank, :], fl[:, lanes], 1, 0)
            return part[:, :xrows].T, part[:, xrows:].T

        def space_part(m):
            lanes = pl.ds(m * half, half)
            pair = dot(fh[:, lanes], b_ref[lanes, rank : 3 * rank], 1, 0)
            return pair[:, :rank] + pair[:, rank:] + dot(fl[:, lanes], b_ref[lanes, :rank], 1, 0)

        def send_core(m, parts):
            for j in range(2):
                tp[it, 2 * m + j] = parts[j]
            two = pl.ds(2 * m, 2)
            put(tp.at[it, two], cr.at[it, two], it, m, at(1 - c, x, y), z)

        def send_x(m, parts):
            drain(cr.at[it, pl.ds(2 * m, 2)], recv, it, m)
            for j in (2 * m, 2 * m + 1):
                th[it, j] = parts[j % 2] + cr[it, j]
                d = ORDER[j]
                if d:
                    put(th.at[it, j], xr.at[it, d - 1], it, X_SUM, at(c, (x + d) % NX, y), z)

        def arrive(m):
            if it == 0:
                sig_load[2 * m].wait()
                sig_load[2 * m + 1].wait()

        mis = jnp.zeros((8, 128), F32)
        rebuild(0)
        arrive(0)
        rebuild(1)
        mis = respond(0, mis)
        arrive(1)
        rebuild(2)
        mis = respond(1, mis)
        parts = time_part(0)
        if it == 0:
            pl.semaphore_wait(barrier, len(cx_peers) + len(y_peers) + len(z_peers))
        send_core(0, parts)
        arrive(2)
        rebuild(3)
        mis = respond(2, mis)
        send_core(1, time_part(1))
        arrive(3)
        mis = respond(3, mis)
        parts = time_part(2)
        sp[it] = space_part(0)
        send_x(0, parts)
        send_x(1, time_part(3))
        sp[it] = sp[it] + space_part(1)
        for d, zz in enumerate(z_peers):
            rows = pl.ds(pl.multiple_of(zz * zrows, zrows), zrows)
            put(sp.at[it, rows, :], zr.at[it, d], it, Z_SUM, p, zz)
        drain(xr.at[it], recv, it, X_SUM)
        ts[it] = th[it, NX - 1] + xr[it, 0] + xr[it, 1] + xr[it, 2]
        for d, yy in enumerate(y_peers):
            rows = pl.ds(pl.multiple_of(yy * yrows, yrows), yrows)
            put(ts.at[it, rows, :], yr.at[it, d], it, Y_SUM, at(c, x, yy), z)
        if it == 0:
            for cp in inv_loads:
                cp.wait()
        drain(zr.at[it], recv, it, Z_SUM)
        own_z = pl.ds(pl.multiple_of(z * zrows, zrows), zrows)
        piece = sp[it, own_z, :]
        for d in range(nz - 1):
            piece = piece + zr[it, d]
        if it > 0:
            piece = piece * scale_u
        s_raw = jnp.dot(piece, inv_s[...], precision=lax.Precision.HIGHEST, preferred_element_type=F32)
        s_nx[it, own_z, :] = s_raw
        for zz in z_peers:
            put(s_nx.at[it, own_z, :], s_nx.at[it, own_z, :], it, Z_ALL, p, zz)
        s_sq = jnp.sum(s_raw * s_raw, axis=0, keepdims=True)

        drain(yr.at[it], recv, it, Y_SUM)
        rows = pl.ds(pl.multiple_of(y * yrows, yrows), yrows)
        piece = ts[it, rows, :]
        for d in range(NY - 1):
            piece = piece + yr[it, d]
        piece = piece * (math.sqrt(rank) if it == 0 else math.sqrt(rank) / scale_u)
        t_raw = jnp.dot(piece, inv_t[...], precision=lax.Precision.HIGHEST, preferred_element_type=F32)
        own_t = pl.ds(pl.multiple_of(c * half + x * xrows + y * yrows, yrows), yrows)
        u_nx[it, own_t, :] = t_raw
        t_sq = jnp.sum(t_raw * t_raw, axis=0, keepdims=True)

        mis = jnp.sum(mis, axis=0, keepdims=True)
        row = lax.broadcasted_iota(jnp.int32, (8, 128), 0)
        vec = jnp.where(row == 0, s_sq, jnp.where(row == 1, t_sq, jnp.where(row == 2, mis, 0.0)))
        me = c * NX + x
        nv[it, 0, me] = vec
        for cc, xx in cx_peers:
            put(nv.at[it, 0, me], nv.at[it, 0, me], it, N_CX, at(cc, xx, y), z)
        for yy in y_peers:
            put(u_nx.at[it, own_t, :], u_nx.at[it, own_t, :], it, Y_ALL, at(c, x, yy), z)

        drain(nv.at[it, 0, pl.ds(0, 7)], recv, it, N_CX)
        vec = nv[it, 0, 0]
        for k in range(1, NC * NX):
            vec = vec + nv[it, 0, k]
        nv[it, 1, y] = vec
        for yy in y_peers:
            put(nv.at[it, 1, y], nv.at[it, 1, y], it, N_Y, at(c, x, yy), z)

        drain(yr.at[it], recv, it, Y_ALL)
        own_x = pl.ds(pl.multiple_of(c * half + x * xrows, xrows), xrows)
        for d in ORDER[: NX - 1]:
            put(u_nx.at[it, own_x, :], u_nx.at[it, own_x, :], it, X_ALL, at(c, (x + d) % NX, y), z)

        drain(nv.at[it, 1, pl.ds(0, 7)], recv, it, N_Y)
        vec = nv[it, 1, 0]
        for k in range(1, NY):
            vec = vec + nv[it, 1, k]
        nv[it, 2, z] = vec
        for zz in z_peers:
            put(nv.at[it, 2, z], nv.at[it, 2, z], it, N_Z, p, zz)

        drain(xr.at[it], recv, it, X_ALL)
        own_c = pl.ds(pl.multiple_of(c * half, half), half)
        put(u_nx.at[it, own_c, :], u_nx.at[it, own_c, :], it, C_ALL, at(1 - c, x, y), z)
        drain(cr.at[it], recv, it, C_ALL)
        if it + 1 < ITERS:
            split_time(u_nx.at[it])
        drain(zr.at[it], recv, it, Z_ALL)
        drain(nv.at[it, 2, pl.ds(0, 7)], recv, it, N_Z)
        vec = nv[it, 2, 0]
        for k in range(1, nz):
            vec = vec + nv[it, 2, k]
        scale_s = 1.0 / jnp.sqrt(vec[0:1, :] / point_total + 1e-6)
        scale_u = 1.0 / jnp.sqrt(vec[1:2, :] / moment_total + 1e-6)
        mis_out[it : it + 1, :] = vec[2:3, :] / (point_total * moment_total)

    s_out[...] = s_nx[ITERS - 1] * scale_s
    u_out[...] = u_nx[ITERS - 1] * scale_u
    for it in range(ITERS):
        for m in range(2):
            drain(cr.at[it, pl.ds(2 * m, 2)], send, it, m)
        small = nv.at[it, 0, pl.ds(0, 7)]
        for stage, ref in (
            (X_SUM, xr.at[it]), (Y_SUM, yr.at[it]), (Z_SUM, zr.at[it]), (Z_ALL, zr.at[it]), (Y_ALL, yr.at[it]),
            (X_ALL, xr.at[it]), (C_ALL, cr.at[it]), (N_CX, small), (N_Y, small), (N_Z, small),
        ):
            drain(ref, send, it, stage)


def store(s, u, mis, s_out, u_out, mis_out, sem):
    copies = [pltpu.make_async_copy(u, u_out, sem.at[0]), pltpu.make_async_copy(s, s_out, sem.at[1])]
    for cp in copies:
        cp.start()
    for k in range(ITERS):
        mis_out[k] = jnp.sum(mis[k : k + 1, :])
    for cp in copies:
        cp.wait()


def shards(nz, s0, u0, sig, rate, power, inv_s, inv_t):
    points, rank = s0.shape
    moments = u0.shape[0]
    half = moments // NC
    xrows = half // NX
    yrows = xrows // NY
    zrows = points // nz
    blocks = moments // xrows
    vmem, smem = pl.BlockSpec(memory_space=pltpu.VMEM), pl.BlockSpec(memory_space=pltpu.SMEM)
    hbm = pl.BlockSpec(memory_space=pltpu.HBM)
    outs = (
        jax.ShapeDtypeStruct((points, rank), F32),
        jax.ShapeDtypeStruct((moments, rank), F32),
        jax.ShapeDtypeStruct((ITERS,), F32),
    )
    modes = pl.pallas_call(
        functools.partial(kernel, nz),
        out_shape=outs[:2] + (jax.ShapeDtypeStruct((ITERS, 128), F32),),
        in_specs=[hbm] * 7,
        out_specs=(vmem, vmem, vmem),
        scratch_shapes=[
            pltpu.VMEM((points, rank), F32),
            pltpu.VMEM((moments, rank), F32),
            pltpu.VMEM((blocks, points, xrows), F32),
            pltpu.VMEM((points // 128, 128), F32),
            pltpu.VMEM((points // 128, 128), F32),
            pltpu.VMEM((rank, rank), F32),
            pltpu.VMEM((rank, rank), F32),
            pltpu.VMEM((points, 128), F32),
            pltpu.VMEM((points, 128), F32),
            pltpu.VMEM((points, 2 * rank), BF16),
            pltpu.VMEM((2 * rank, points), BF16),
            pltpu.VMEM((moments, 4 * rank), BF16),
            pltpu.VMEM((2, points, 2 * xrows), F32),
            pltpu.VMEM((points, moments), BF16),
            pltpu.VMEM((points, moments), BF16),
            pltpu.VMEM((ITERS, NX, xrows, rank), F32),
            pltpu.VMEM((ITERS, NX, xrows, rank), F32),
            pltpu.VMEM((ITERS, NX, xrows, rank), F32),
            pltpu.VMEM((ITERS, NX - 1, xrows, rank), F32),
            pltpu.VMEM((ITERS, xrows, rank), F32),
            pltpu.VMEM((ITERS, NY - 1, yrows, rank), F32),
            pltpu.VMEM((ITERS, moments, rank), F32),
            pltpu.VMEM((ITERS, points, rank), F32),
            pltpu.VMEM((ITERS, nz - 1, zrows, rank), F32),
            pltpu.VMEM((ITERS, points, rank), F32),
            pltpu.VMEM((ITERS, 3, 8, 8, 128), F32),
            pltpu.SemaphoreType.DMA((6 + blocks,)),
            pltpu.SemaphoreType.DMA((ITERS, STAGES)),
            pltpu.SemaphoreType.DMA((ITERS, STAGES)),
        ],
        compiler_params=pltpu.CompilerParams(
            collective_id=0, has_side_effects=True, vmem_limit_bytes=40 * 1024 * 1024
        ),
    )(*[pltpu.with_memory_space_constraint(v, pltpu.HBM) for v in (
        s0, u0, sig, rate.reshape(points // 128, 128), power.reshape(points // 128, 128), inv_s, inv_t)])
    return pl.pallas_call(
        store,
        out_shape=outs,
        in_specs=[vmem, vmem, vmem],
        out_specs=(hbm, hbm, smem),
        scratch_shapes=[pltpu.SemaphoreType.DMA((2,))],
    )(*[pltpu.with_memory_space_constraint(v, pltpu.VMEM) for v in modes])


def solution(mesh):
    return jax.shard_map(
        functools.partial(shards, mesh.shape["tm"]),
        mesh=mesh,
        in_specs=(P("pts", None), P("tm", None), P("pts", "tm"), P("pts"), P("pts"), P(), P()),
        out_specs=(P("pts", None), P("tm", None), P()),
        check_vma=False,
    )
```

time: 82 us -> 67.8 us (0.83); the launches traced: 80.4 us -> 67.7 us
  local copies, waits for them, and re-layouts: 8.62 us -> 0 us
  Pallas kernels: 71.1 us -> 67.1 us
    unnamed x17 -> x0, local copies, waits for them, and re-layouts: 8.62 us -> none
    pallas_call x1 -> x2, Pallas kernels: 71.1 us -> 67.1 us  [the longest x1 65.6 us: shards(): pl.pallas_call(functools.partial(kernel, nz), out_shape=outs[:2] + (jax.S...]
where the time goes in v2:
time: 67.8 us; the launch traced here: 67.7 us
  Pallas kernels  67.1 us (99%)
    pallas_call x1, Pallas kernels, shards(): pl.pallas_call(functools.partial(kernel, nz), out_shape=outs[:2] + (jax.S...  65.6 us
    pallas_call x1, Pallas kernels, shards(): pl.pallas_call(store, out_shape=outs, in_specs=[vmem, vmem, vmem], out_sp...  1.41 us

profile of v2, /device:TPU:1, one launch (start us, length us, event | category | flops | bytes accessed | tf_op | source)
XLA Modules:
  0.0 67.7 jit_solution(8777359951240910264)
XLA Ops:
  0.6 65.6 %shard_map.94 = (f32[512,128]{1,0:T(8,128)S(1)}, f32[1024,128]{1,0:T(8,128)S(1)}, f32[2,128]{1,0:T(2,128)S(1)}) custom-call(f32[512,128]{1,0:T(8,128)} %s_in.1, f32[1024,128]{1,0:T(8,128)} %u_in.1, f32[512,1024]{1,0:T(8,128)} %sig_in.1, f32[4,128]{1,0:T(4,128)} %bitcast.2, f32[4,128]{1,0:T(4,128)} %bitcast.3, f32[128,128]{1,0:T(8,128)} %inv_s_in.1, ...), custom_call_target="tpu_custom_call" | custom-call | tf_op jit(solution)/shard_map/pallas_call | solution.py:314
  66.3 1.4 %shard_map.95 = (f32[512,128]{1,0:T(8,128)}, f32[1024,128]{1,0:T(8,128)}, f32[2]{0:T(128)}) custom-call(f32[512,128]{1,0:T(8,128)S(1)} %get-tuple-element.6.s, f32[1024,128]{1,0:T(8,128)S(1)} %get-tuple-element.7.u, f32[2,128]{1,0:T(2,128)S(1)} %get-tuple-element.8.mis), custom_call_target="tpu_custom_call" | custom-call | tf_op jit(solution)/shard_map/pallas_call | solution.py:355

commit v3 on v2

--- a/solution.py
+++ b/solution.py
@@ -13,7 +13,10 @@
 MESH = pl.DeviceIdType.MESH
 NX, NY, NC = 4, 8, 2
 ORDER = (2, 1, 3, 0)
-X_SUM, Y_SUM, Z_SUM, Z_ALL, Y_ALL, X_ALL, C_ALL, N_CX, N_Y, N_Z, STAGES = range(2, 13)
+NEAR = (1, 7, 2, 6, 3, 5, 4)
+X_SUM, Y_SUM, Z_SUM, Z_ALL, C_ALL, N_XY, N_Z, M_CX, M_Y, M_Z, Y_ALL = range(2, 13)
+X_ALL = Y_ALL + NY
+STAGES = X_ALL + NY
 
 
 def split(value):
@@ -27,7 +30,7 @@
 
 def kernel(nz, s_in, u_in, sig_in, rate_in, power_in, inv_s_in, inv_t_in, s_out, u_out, mis_out,
            s0, u0, sig, rate, power, inv_s, inv_t,
-           lr, ex, a_ref, at_ref, b_ref, rec, fh, fl, tp, cr, th, xr, ts, yr, u_nx, sp, zr, s_nx, nv,
+           sig_lr, sig_ex, lr, ex, a_ref, at_ref, b_ref, rec, fh, fl, tp, cr, th, xr, ts, yr, u_nx, sp, zr, s_nx, nv, n_xy, n_z,
            load, send, recv):
     points, rank = s0.shape
     moments = u0.shape[0]
@@ -49,8 +52,16 @@
         for dx in range(NX):
             if dc or dx:
                 cx_peers.append(((c + dc) % NC, (x + dx) % NX))
-    y_peers = [(y + d) % NY for d in range(1, NY)]
-    z_peers = [(z + d) % nz for d in range(1, nz)]
+    y_peers = [(y + d) % NY for d in NEAR[::-1]]
+    z_far = sorted(range(1, nz), key=lambda d: -min(d, nz - d))
+    z_peers = [(z + d) % nz for d in z_far]
+    turned = [pl.multiple_of(zz * zrows, zrows) for zz in z_peers + [z]]
+    plane = []
+    for dy in NEAR[::-1] + (0,):
+        for dx in ORDER:
+            for dc in (1, 0):
+                if dc or dx or dy:
+                    plane.append(at((c + dc) % NC, (x + dx) % NX, (y + dy) % NY))
 
     starts = []
     for side in (1 - c, c):
@@ -71,10 +82,8 @@
     inv_loads = [fetch(inv_s_in, inv_s), fetch(inv_t_in, inv_t)]
 
     barrier = pltpu.get_barrier_semaphore()
-    for cc, xx in cx_peers:
-        pl.semaphore_signal(barrier, inc=1, device_id=(at(cc, xx, y), z), device_id_type=MESH)
-    for yy in y_peers:
-        pl.semaphore_signal(barrier, inc=1, device_id=(at(c, x, yy), z), device_id_type=MESH)
+    for pp in plane:
+        pl.semaphore_signal(barrier, inc=1, device_id=(pp, z), device_id_type=MESH)
     for zz in z_peers:
         pl.semaphore_signal(barrier, inc=1, device_id=(p, zz), device_id_type=MESH)
 
@@ -87,8 +96,9 @@
     def drain(ref, sem, it, stage):
         pltpu.make_async_copy(ref, ref, sem.at[it, stage]).wait()
 
-    def split_time(u_cur):
-        for k, q in enumerate(starts):
+    def split_time(u_cur, slots):
+        for k in slots:
+            q = starts[k]
             rows = pl.ds(k * xrows, xrows)
             hi, lo = split(u_cur[pl.ds(q, xrows), :])
             b_ref[rows, :rank] = hi
@@ -96,14 +106,24 @@
             b_ref[rows, 2 * rank : 3 * rank] = lo
             b_ref[rows, 3 * rank :] = lo
 
+    def total(ref, count):
+        sums = [ref[k] for k in range(4)]
+        for k in range(4, count):
+            sums[k % 4] = sums[k % 4] + ref[k]
+        return (sums[0] + sums[1]) + (sums[2] + sums[3])
+
     rate_load.wait()
     power_load.wait()
     for k in range(points // 128):
         rows = pl.ds(k * 128, 128)
-        lr[rows, :] = jnp.broadcast_to(jnp.log2(rate[k : k + 1, :]), (128, 128)).T
-        ex[rows, :] = jnp.broadcast_to(0.5 * (power[k : k + 1, :] - 1.0), (128, 128)).T
+        sig_lr[rows, :] = jnp.broadcast_to(jnp.log2(rate[k : k + 1, :]), (128, 128)).T
+        sig_ex[rows, :] = jnp.broadcast_to(0.5 * (power[k : k + 1, :] - 1.0), (128, 128)).T
+    for r, q in enumerate(turned):
+        rows = pl.ds(r * zrows, zrows)
+        lr[rows, :] = sig_lr[pl.ds(q, zrows), :]
+        ex[rows, :] = sig_ex[pl.ds(q, zrows), :]
     u_load.wait()
-    split_time(u0)
+    split_time(u0, range(blocks))
     s_load.wait()
 
     scale_s = scale_u = None
@@ -111,9 +131,9 @@
         s_cur = s0 if it == 0 else s_nx.at[it - 1]
         root = 1.0 / math.sqrt(rank)
         factor = root if it == 0 else scale_s * scale_u * root
-        for k in range(points // 128):
-            rows = pl.ds(k * 128, 128)
-            sv = s_cur[rows, :] * factor
+        for k in range(nz // 2):
+            rows = pl.ds(2 * k * zrows, 2 * zrows)
+            sv = jnp.concatenate([s_cur[pl.ds(q, zrows), :] for q in turned[2 * k : 2 * k + 2]], axis=0) * factor
             hi, lo = split(sv)
             a_ref[rows, :rank] = hi
             a_ref[rows, rank:] = lo
@@ -123,16 +143,18 @@
 
         def rebuild(m):
             rows = pl.ds(2 * m * xrows, 2 * xrows)
-            rec[m % 2] = dot(a_ref[...], b_ref[rows, : 2 * rank], 1, 1) + dot(a_ref[...], b_ref[rows, 2 * rank :], 1, 1)
+            for pts in (pl.ds(0, points // 2), pl.ds(points // 2, points // 2)):
+                rec[m % 2, pts, :] = dot(a_ref[pts, :], b_ref[rows, : 2 * rank], 1, 1) + dot(
+                    a_ref[pts, :], b_ref[rows, 2 * rank :], 1, 1)
 
         def respond(m, mis):
             for k in (2 * m, 2 * m + 1):
                 lanes = pl.ds(k * xrows, xrows)
-                for r in range(points // 64):
-                    rows = pl.ds(r * 64, 64)
-                    stress = sig[k, rows, :] - rec[m % 2, rows, pl.ds((k % 2) * xrows, xrows)]
+                for r, q in enumerate(turned):
+                    rows = pl.ds(r * zrows, zrows)
+                    stress = sig[k, pl.ds(q, zrows), :] - rec[m % 2, rows, pl.ds((k % 2) * xrows, xrows)]
                     quad = stress * stress
-                    mis = mis + jnp.sum(quad.reshape(8, 8, 128), axis=0)
+                    mis = mis + jnp.sum(quad.reshape(zrows // 8, 8, 128), axis=0)
                     flow = stress * jnp.exp2(lr[rows, :] + ex[rows, :] * jnp.log2(quad + 1e-6))
                     hi, lo = split(flow)
                     fh[rows, lanes] = hi
@@ -145,10 +167,12 @@
             part = pair[:rank] + pair[rank:] + dot(at_ref[:rank, :], fl[:, lanes], 1, 0)
             return part[:, :xrows].T, part[:, xrows:].T
 
-        def space_part(m):
-            lanes = pl.ds(m * half, half)
-            pair = dot(fh[:, lanes], b_ref[lanes, rank : 3 * rank], 1, 0)
-            return pair[:, :rank] + pair[:, rank:] + dot(fl[:, lanes], b_ref[lanes, :rank], 1, 0)
+        def send_space(h):
+            pts = pl.ds(h * (points // 2), points // 2)
+            pair = dot(fh[pts, :], b_ref[:, rank : 3 * rank], 1, 0)
+            sp[it, pts, :] = pair[:, :rank] + pair[:, rank:] + dot(fl[pts, :], b_ref[:, :rank], 1, 0)
+            for r in range(h * nz // 2, min((h + 1) * nz // 2, nz - 1)):
+                put(sp.at[it, pl.ds(r * zrows, zrows), :], zr.at[it, r], it, Z_SUM, p, z_peers[r])
 
         def send_core(m, parts):
             for j in range(2):
@@ -174,27 +198,28 @@
         arrive(0)
         rebuild(1)
         mis = respond(0, mis)
+        parts = time_part(0)
+        if it == 0:
+            pl.semaphore_wait(barrier, len(plane) + len(z_peers))
+        send_core(0, parts)
         arrive(1)
         rebuild(2)
         mis = respond(1, mis)
-        parts = time_part(0)
-        if it == 0:
-            pl.semaphore_wait(barrier, len(cx_peers) + len(y_peers) + len(z_peers))
-        send_core(0, parts)
+        send_core(1, time_part(1))
         arrive(2)
         rebuild(3)
         mis = respond(2, mis)
-        send_core(1, time_part(1))
+        send_x(0, time_part(2))
         arrive(3)
         mis = respond(3, mis)
-        parts = time_part(2)
-        sp[it] = space_part(0)
-        send_x(0, parts)
         send_x(1, time_part(3))
-        sp[it] = sp[it] + space_part(1)
-        for d, zz in enumerate(z_peers):
-            rows = pl.ds(pl.multiple_of(zz * zrows, zrows), zrows)
-            put(sp.at[it, rows, :], zr.at[it, d], it, Z_SUM, p, zz)
+        send_space(0)
+        send_space(1)
+        me = c * NX + x
+        nv[it, 0, me] = jnp.sum(mis, axis=0, keepdims=True)
+        for cc, xx in cx_peers:
+            put(nv.at[it, 0, me], nv.at[it, 0, me], it, M_CX, at(cc, xx, y), z)
+
         drain(xr.at[it], recv, it, X_SUM)
         ts[it] = th[it, NX - 1] + xr[it, 0] + xr[it, 1] + xr[it, 2]
         for d, yy in enumerate(y_peers):
@@ -203,18 +228,37 @@
         if it == 0:
             for cp in inv_loads:
                 cp.wait()
+        drain(nv.at[it, 0, pl.ds(0, 7)], recv, it, M_CX)
+        nv[it, 1, y] = total(nv.at[it, 0], NC * NX)
+        for yy in y_peers:
+            put(nv.at[it, 1, y], nv.at[it, 1, y], it, M_Y, at(c, x, yy), z)
+
+        def piece_rows(xx, yy):
+            return pl.ds(pl.multiple_of(c * half + xx * xrows + yy * yrows, yrows), yrows)
+
+        def pass_x(dy):
+            rows = piece_rows(x, (y + NY - dy) % NY)
+            for d in ORDER[: NX - 1]:
+                put(u_nx.at[it, rows, :], u_nx.at[it, rows, :], it, X_ALL + dy, at(c, (x + d) % NX, y), z)
+
+        def pass_core(dy):
+            drain(xr.at[it, 0, pl.ds(0, (NX - 1) * yrows)], recv, it, X_ALL + dy)
+            for d in ORDER[: NX - 1]:
+                rows = piece_rows((x + d) % NX, (y + NY - dy) % NY)
+                put(u_nx.at[it, rows, :], u_nx.at[it, rows, :], it, C_ALL, at(1 - c, x, y), z)
+
         drain(zr.at[it], recv, it, Z_SUM)
         own_z = pl.ds(pl.multiple_of(z * zrows, zrows), zrows)
-        piece = sp[it, own_z, :]
+        piece = sp[it, pl.ds((nz - 1) * zrows, zrows), :]
         for d in range(nz - 1):
             piece = piece + zr[it, d]
         if it > 0:
             piece = piece * scale_u
         s_raw = jnp.dot(piece, inv_s[...], precision=lax.Precision.HIGHEST, preferred_element_type=F32)
         s_nx[it, own_z, :] = s_raw
+        n_xy[it, p, :, :rank] = jnp.sum(s_raw * s_raw, axis=0, keepdims=True)
         for zz in z_peers:
             put(s_nx.at[it, own_z, :], s_nx.at[it, own_z, :], it, Z_ALL, p, zz)
-        s_sq = jnp.sum(s_raw * s_raw, axis=0, keepdims=True)
 
         drain(yr.at[it], recv, it, Y_SUM)
         rows = pl.ds(pl.multiple_of(y * yrows, yrows), yrows)
@@ -223,55 +267,45 @@
             piece = piece + yr[it, d]
         piece = piece * (math.sqrt(rank) if it == 0 else math.sqrt(rank) / scale_u)
         t_raw = jnp.dot(piece, inv_t[...], precision=lax.Precision.HIGHEST, preferred_element_type=F32)
-        own_t = pl.ds(pl.multiple_of(c * half + x * xrows + y * yrows, yrows), yrows)
+        own_t = piece_rows(x, y)
         u_nx[it, own_t, :] = t_raw
-        t_sq = jnp.sum(t_raw * t_raw, axis=0, keepdims=True)
-
-        mis = jnp.sum(mis, axis=0, keepdims=True)
-        row = lax.broadcasted_iota(jnp.int32, (8, 128), 0)
-        vec = jnp.where(row == 0, s_sq, jnp.where(row == 1, t_sq, jnp.where(row == 2, mis, 0.0)))
-        me = c * NX + x
-        nv[it, 0, me] = vec
-        for cc, xx in cx_peers:
-            put(nv.at[it, 0, me], nv.at[it, 0, me], it, N_CX, at(cc, xx, y), z)
-        for yy in y_peers:
-            put(u_nx.at[it, own_t, :], u_nx.at[it, own_t, :], it, Y_ALL, at(c, x, yy), z)
-
-        drain(nv.at[it, 0, pl.ds(0, 7)], recv, it, N_CX)
-        vec = nv[it, 0, 0]
-        for k in range(1, NC * NX):
-            vec = vec + nv[it, 0, k]
-        nv[it, 1, y] = vec
-        for yy in y_peers:
-            put(nv.at[it, 1, y], nv.at[it, 1, y], it, N_Y, at(c, x, yy), z)
-
-        drain(yr.at[it], recv, it, Y_ALL)
-        own_x = pl.ds(pl.multiple_of(c * half + x * xrows, xrows), xrows)
-        for d in ORDER[: NX - 1]:
-            put(u_nx.at[it, own_x, :], u_nx.at[it, own_x, :], it, X_ALL, at(c, (x + d) % NX, y), z)
-
-        drain(nv.at[it, 1, pl.ds(0, 7)], recv, it, N_Y)
-        vec = nv[it, 1, 0]
-        for k in range(1, NY):
-            vec = vec + nv[it, 1, k]
-        nv[it, 2, z] = vec
+        n_xy[it, p, :, rank:] = jnp.sum(t_raw * t_raw, axis=0, keepdims=True)
+        for pp in plane:
+            put(n_xy.at[it, p], n_xy.at[it, p], it, N_XY, pp, z)
+        for d in NEAR[::-1]:
+            put(u_nx.at[it, own_t, :], u_nx.at[it, own_t, :], it, Y_ALL + d, at(c, x, (y + d) % NY), z)
+        pass_x(0)
+
+        drain(nv.at[it, 1, pl.ds(0, 7)], recv, it, M_Y)
+        nv[it, 2, z] = total(nv.at[it, 1], NY)
         for zz in z_peers:
-            put(nv.at[it, 2, z], nv.at[it, 2, z], it, N_Z, p, zz)
-
-        drain(xr.at[it], recv, it, X_ALL)
-        own_c = pl.ds(pl.multiple_of(c * half, half), half)
-        put(u_nx.at[it, own_c, :], u_nx.at[it, own_c, :], it, C_ALL, at(1 - c, x, y), z)
+            put(nv.at[it, 2, z], nv.at[it, 2, z], it, M_Z, p, zz)
+
+        for d in NEAR:
+            drain(u_nx.at[it, piece_rows(x, (y + NY - d) % NY), :], recv, it, Y_ALL + d)
+            pass_x(d)
+        drain(n_xy.at[it, pl.ds(0, len(plane))], recv, it, N_XY)
+        n_z[it, z] = total(n_xy.at[it], len(plane) + 1)
+        for zz in z_peers:
+            put(n_z.at[it, z], n_z.at[it, z], it, N_Z, p, zz)
+        own = pl.ds(pl.multiple_of(c * half + x * xrows, xrows), xrows)
+        put(u_nx.at[it, own, :], u_nx.at[it, own, :], it, C_ALL, at(1 - c, x, y), z)
+        for d in (0,) + NEAR[:2]:
+            pass_core(d)
+        for d in NEAR[2:]:
+            pass_core(d)
+        if it + 1 < ITERS:
+            split_time(u_nx.at[it], range(NX, 2 * NX))
         drain(cr.at[it], recv, it, C_ALL)
         if it + 1 < ITERS:
-            split_time(u_nx.at[it])
+            split_time(u_nx.at[it], range(NX))
         drain(zr.at[it], recv, it, Z_ALL)
-        drain(nv.at[it, 2, pl.ds(0, 7)], recv, it, N_Z)
-        vec = nv[it, 2, 0]
-        for k in range(1, nz):
-            vec = vec + nv[it, 2, k]
-        scale_s = 1.0 / jnp.sqrt(vec[0:1, :] / point_total + 1e-6)
-        scale_u = 1.0 / jnp.sqrt(vec[1:2, :] / moment_total + 1e-6)
-        mis_out[it : it + 1, :] = vec[2:3, :] / (point_total * moment_total)
+        drain(nv.at[it, 2, pl.ds(0, 7)], recv, it, M_Z)
+        mis_out[it] = total(nv.at[it, 2], nz) / (point_total * moment_total)
+        drain(n_z.at[it, pl.ds(0, nz - 1)], recv, it, N_Z)
+        quads = total(n_z.at[it], nz)
+        scale_s = 1.0 / jnp.sqrt(quads[:, :rank] / point_total + 1e-6)
+        scale_u = 1.0 / jnp.sqrt(quads[:, rank:] / moment_total + 1e-6)
 
     s_out[...] = s_nx[ITERS - 1] * scale_s
     u_out[...] = u_nx[ITERS - 1] * scale_u
@@ -280,10 +314,15 @@
             drain(cr.at[it, pl.ds(2 * m, 2)], send, it, m)
         small = nv.at[it, 0, pl.ds(0, 7)]
         for stage, ref in (
-            (X_SUM, xr.at[it]), (Y_SUM, yr.at[it]), (Z_SUM, zr.at[it]), (Z_ALL, zr.at[it]), (Y_ALL, yr.at[it]),
-            (X_ALL, xr.at[it]), (C_ALL, cr.at[it]), (N_CX, small), (N_Y, small), (N_Z, small),
+            (X_SUM, xr.at[it]), (Y_SUM, yr.at[it]), (Z_SUM, zr.at[it]), (Z_ALL, zr.at[it]),
+            (C_ALL, cr.at[it]), (M_CX, small), (M_Y, small), (M_Z, small),
+            (N_XY, n_xy.at[it, pl.ds(0, len(plane))]), (N_Z, n_z.at[it, pl.ds(0, nz - 1)]),
         ):
             drain(ref, send, it, stage)
+        for d in NEAR:
+            drain(yr.at[it, 0], send, it, Y_ALL + d)
+        for d in range(NY):
+            drain(xr.at[it, 0, pl.ds(0, (NX - 1) * yrows)], send, it, X_ALL + d)
 
 
 def store(s, u, mis, s_out, u_out, mis_out, sem):
@@ -291,7 +330,7 @@
     for cp in copies:
         cp.start()
     for k in range(ITERS):
-        mis_out[k] = jnp.sum(mis[k : k + 1, :])
+        mis_out[k] = jnp.sum(mis[k])
     for cp in copies:
         cp.wait()
 
@@ -313,7 +352,7 @@
     )
     modes = pl.pallas_call(
         functools.partial(kernel, nz),
-        out_shape=outs[:2] + (jax.ShapeDtypeStruct((ITERS, 128), F32),),
+        out_shape=outs[:2] + (jax.ShapeDtypeStruct((ITERS, 1, 128), F32),),
         in_specs=[hbm] * 7,
         out_specs=(vmem, vmem, vmem),
         scratch_shapes=[
@@ -324,6 +363,8 @@
             pltpu.VMEM((points // 128, 128), F32),
             pltpu.VMEM((rank, rank), F32),
             pltpu.VMEM((rank, rank), F32),
+            pltpu.VMEM((points, 128), F32),
+            pltpu.VMEM((points, 128), F32),
             pltpu.VMEM((points, 128), F32),
             pltpu.VMEM((points, 128), F32),
             pltpu.VMEM((points, 2 * rank), BF16),
@@ -342,7 +383,9 @@
             pltpu.VMEM((ITERS, points, rank), F32),
             pltpu.VMEM((ITERS, nz - 1, zrows, rank), F32),
             pltpu.VMEM((ITERS, points, rank), F32),
-            pltpu.VMEM((ITERS, 3, 8, 8, 128), F32),
+            pltpu.VMEM((ITERS, 3, 8, 1, 128), F32),
+            pltpu.VMEM((ITERS, NX * NY * NC, 1, 2 * rank), F32),
+            pltpu.VMEM((ITERS, nz, 1, 2 * rank), F32),
             pltpu.SemaphoreType.DMA((6 + blocks,)),
             pltpu.SemaphoreType.DMA((ITERS, STAGES)),
             pltpu.SemaphoreType.DMA((ITERS, STAGES)),

time: 67.8 us -> 64.9 us (0.957)
  Pallas kernels: 67.1 us -> 64.1 us
    pallas_call x1, Pallas kernels: 65.6 us -> 62.7 us  [shards(): pl.pallas_call(functools.partial(kernel, nz), out_shape=outs[:2] + (jax.S...]
where the time goes in v3:
time: 64.9 us; the launch traced here: 64.7 us
  Pallas kernels  64.1 us (99%)
    pallas_call x1, Pallas kernels, shards(): pl.pallas_call(functools.partial(kernel, nz), out_shape=outs[:2] + (jax.S...  62.7 us
    pallas_call x1, Pallas kernels, shards(): pl.pallas_call(store, out_shape=outs, in_specs=[vmem, vmem, vmem], out_sp...  1.41 us

profile of v3, /device:TPU:1, one launch (start us, length us, event | category | flops | bytes accessed | tf_op | source)
XLA Modules:
  0.0 64.7 jit_solution(5223891393897475097)
XLA Ops:
  0.6 62.7 %shard_map.94 = (f32[512,128]{1,0:T(8,128)S(1)}, f32[1024,128]{1,0:T(8,128)S(1)}, f32[2,1,128]{2,1,0:T(1,128)S(1)}) custom-call(f32[512,128]{1,0:T(8,128)} %s_in.1, f32[1024,128]{1,0:T(8,128)} %u_in.1, f32[512,1024]{1,0:T(8,128)} %sig_in.1, f32[4,128]{1,0:T(4,128)} %bitcast.2, f32[4,128]{1,0:T(4,128)} %bitcast.3, f32[128,128]{1,0:T(8,128)} %inv_s_in.1, ...), custom_call_target="tpu_custom_call" | custom-call | tf_op jit(solution)/shard_map/pallas_call | solution.py:353
  63.3 1.4 %shard_map.95 = (f32[512,128]{1,0:T(8,128)}, f32[1024,128]{1,0:T(8,128)}, f32[2]{0:T(128)}) custom-call(f32[512,128]{1,0:T(8,128)S(1)} %get-tuple-element.6.s, f32[1024,128]{1,0:T(8,128)S(1)} %get-tuple-element.7.u, f32[2,1,128]{2,1,0:T(1,128)S(1)} %get-tuple-element.8.mis), custom_call_target="tpu_custom_call" | custom-call | tf_op jit(solution)/shard_map/pallas_call | solution.py:398

commit v4 on v3

--- a/solution.py
+++ b/solution.py
@@ -78,8 +78,10 @@
 
     u_load, s_load = fetch(u_in, u0), fetch(s_in, s0)
     rate_load, power_load = fetch(rate_in, rate), fetch(power_in, power)
-    sig_load = [fetch(sig_in.at[:, pl.ds(q, xrows)], sig.at[k]) for k, q in enumerate(starts)]
-    inv_loads = [fetch(inv_s_in, inv_s), fetch(inv_t_in, inv_t)]
+    def fetch_stress(slots):
+        return [fetch(sig_in.at[:, pl.ds(starts[k], xrows)], sig.at[k]) for k in slots]
+
+    sig_load = fetch_stress(range(2))
 
     barrier = pltpu.get_barrier_semaphore()
     for pp in plane:
@@ -123,6 +125,8 @@
         lr[rows, :] = sig_lr[pl.ds(q, zrows), :]
         ex[rows, :] = sig_ex[pl.ds(q, zrows), :]
     u_load.wait()
+    sig_load += fetch_stress(range(2, blocks))
+    inv_loads = [fetch(inv_s_in, inv_s), fetch(inv_t_in, inv_t)]
     split_time(u0, range(blocks))
     s_load.wait()
 
@@ -131,15 +135,21 @@
         s_cur = s0 if it == 0 else s_nx.at[it - 1]
         root = 1.0 / math.sqrt(rank)
         factor = root if it == 0 else scale_s * scale_u * root
+        def turned_modes(k):
+            return jnp.concatenate([s_cur[pl.ds(q, zrows), :] for q in turned[2 * k : 2 * k + 2]], axis=0) * factor
+
         for k in range(nz // 2):
             rows = pl.ds(2 * k * zrows, 2 * zrows)
-            sv = jnp.concatenate([s_cur[pl.ds(q, zrows), :] for q in turned[2 * k : 2 * k + 2]], axis=0) * factor
-            hi, lo = split(sv)
+            hi, lo = split(turned_modes(k))
             a_ref[rows, :rank] = hi
             a_ref[rows, rank:] = lo
-            hi, lo = split(sv.T)
-            at_ref[:rank, rows] = hi
-            at_ref[rank:, rows] = lo
+
+        def transpose_modes():
+            for k in range(nz // 2):
+                rows = pl.ds(2 * k * zrows, 2 * zrows)
+                hi, lo = split(turned_modes(k).T)
+                at_ref[:rank, rows] = hi
+                at_ref[rank:, rows] = lo
 
         def rebuild(m):
             rows = pl.ds(2 * m * xrows, 2 * xrows)
@@ -174,9 +184,11 @@
             for r in range(h * nz // 2, min((h + 1) * nz // 2, nz - 1)):
                 put(sp.at[it, pl.ds(r * zrows, zrows), :], zr.at[it, r], it, Z_SUM, p, z_peers[r])
 
-        def send_core(m, parts):
+        def keep_core(m, parts):
             for j in range(2):
                 tp[it, 2 * m + j] = parts[j]
+
+        def send_core(m):
             two = pl.ds(2 * m, 2)
             put(tp.at[it, two], cr.at[it, two], it, m, at(1 - c, x, y), z)
 
@@ -197,28 +209,40 @@
         rebuild(0)
         arrive(0)
         rebuild(1)
+        transpose_modes()
         mis = respond(0, mis)
-        parts = time_part(0)
-        if it == 0:
-            pl.semaphore_wait(barrier, len(plane) + len(z_peers))
-        send_core(0, parts)
+        keep_core(0, time_part(0))
+        if it > 0:
+            send_core(0)
         arrive(1)
         rebuild(2)
         mis = respond(1, mis)
-        send_core(1, time_part(1))
+        keep_core(1, time_part(1))
+        if it > 0:
+            send_core(1)
         arrive(2)
         rebuild(3)
         mis = respond(2, mis)
-        send_x(0, time_part(2))
+        parts = time_part(2)
+        if it > 0:
+            send_x(0, parts)
+        else:
+            pl.semaphore_wait(barrier, len(plane) + len(z_peers))
+            send_core(0)
+            send_core(1)
         arrive(3)
         mis = respond(3, mis)
+        if it == 0:
+            send_x(0, parts)
         send_x(1, time_part(3))
         send_space(0)
         send_space(1)
+        last = it + 1 == ITERS
         me = c * NX + x
-        nv[it, 0, me] = jnp.sum(mis, axis=0, keepdims=True)
-        for cc, xx in cx_peers:
-            put(nv.at[it, 0, me], nv.at[it, 0, me], it, M_CX, at(cc, xx, y), z)
+        nv[0, me, :, it * 128 : (it + 1) * 128] = jnp.sum(mis, axis=0, keepdims=True)
+        if last:
+            for cc, xx in cx_peers:
+                put(nv.at[0, me], nv.at[0, me], it, M_CX, at(cc, xx, y), z)
 
         drain(xr.at[it], recv, it, X_SUM)
         ts[it] = th[it, NX - 1] + xr[it, 0] + xr[it, 1] + xr[it, 2]
@@ -228,10 +252,11 @@
         if it == 0:
             for cp in inv_loads:
                 cp.wait()
-        drain(nv.at[it, 0, pl.ds(0, 7)], recv, it, M_CX)
-        nv[it, 1, y] = total(nv.at[it, 0], NC * NX)
-        for yy in y_peers:
-            put(nv.at[it, 1, y], nv.at[it, 1, y], it, M_Y, at(c, x, yy), z)
+        if last:
+            drain(nv.at[0, pl.ds(0, 7)], recv, it, M_CX)
+            nv[1, y] = total(nv.at[0], NC * NX)
+            for yy in y_peers:
+                put(nv.at[1, y], nv.at[1, y], it, M_Y, at(c, x, yy), z)
 
         def piece_rows(xx, yy):
             return pl.ds(pl.multiple_of(c * half + xx * xrows + yy * yrows, yrows), yrows)
@@ -276,10 +301,11 @@
             put(u_nx.at[it, own_t, :], u_nx.at[it, own_t, :], it, Y_ALL + d, at(c, x, (y + d) % NY), z)
         pass_x(0)
 
-        drain(nv.at[it, 1, pl.ds(0, 7)], recv, it, M_Y)
-        nv[it, 2, z] = total(nv.at[it, 1], NY)
-        for zz in z_peers:
-            put(nv.at[it, 2, z], nv.at[it, 2, z], it, M_Z, p, zz)
+        if last:
+            drain(nv.at[1, pl.ds(0, 7)], recv, it, M_Y)
+            nv[2, z] = total(nv.at[1], NY)
+            for zz in z_peers:
+                put(nv.at[2, z], nv.at[2, z], it, M_Z, p, zz)
 
         for d in NEAR:
             drain(u_nx.at[it, piece_rows(x, (y + NY - d) % NY), :], recv, it, Y_ALL + d)
@@ -300,8 +326,9 @@
         if it + 1 < ITERS:
             split_time(u_nx.at[it], range(NX))
         drain(zr.at[it], recv, it, Z_ALL)
-        drain(nv.at[it, 2, pl.ds(0, 7)], recv, it, M_Z)
-        mis_out[it] = total(nv.at[it, 2], nz) / (point_total * moment_total)
+        if last:
+            drain(nv.at[2, pl.ds(0, 7)], recv, it, M_Z)
+            mis_out[...] = total(nv.at[2], nz) / (point_total * moment_total)
         drain(n_z.at[it, pl.ds(0, nz - 1)], recv, it, N_Z)
         quads = total(n_z.at[it], nz)
         scale_s = 1.0 / jnp.sqrt(quads[:, :rank] / point_total + 1e-6)
@@ -312,13 +339,15 @@
     for it in range(ITERS):
         for m in range(2):
             drain(cr.at[it, pl.ds(2 * m, 2)], send, it, m)
-        small = nv.at[it, 0, pl.ds(0, 7)]
         for stage, ref in (
             (X_SUM, xr.at[it]), (Y_SUM, yr.at[it]), (Z_SUM, zr.at[it]), (Z_ALL, zr.at[it]),
-            (C_ALL, cr.at[it]), (M_CX, small), (M_Y, small), (M_Z, small),
+            (C_ALL, cr.at[it]),
             (N_XY, n_xy.at[it, pl.ds(0, len(plane))]), (N_Z, n_z.at[it, pl.ds(0, nz - 1)]),
         ):
             drain(ref, send, it, stage)
+        if it + 1 == ITERS:
+            for stage in (M_CX, M_Y, M_Z):
+                drain(nv.at[0, pl.ds(0, 7)], send, it, stage)
         for d in NEAR:
             drain(yr.at[it, 0], send, it, Y_ALL + d)
         for d in range(NY):
@@ -330,7 +359,7 @@
     for cp in copies:
         cp.start()
     for k in range(ITERS):
-        mis_out[k] = jnp.sum(mis[k])
+        mis_out[k] = jnp.sum(mis[:, k * 128 : (k + 1) * 128])
     for cp in copies:
         cp.wait()
 
@@ -352,7 +381,7 @@
     )
     modes = pl.pallas_call(
         functools.partial(kernel, nz),
-        out_shape=outs[:2] + (jax.ShapeDtypeStruct((ITERS, 1, 128), F32),),
+        out_shape=outs[:2] + (jax.ShapeDtypeStruct((1, ITERS * 128), F32),),
         in_specs=[hbm] * 7,
         out_specs=(vmem, vmem, vmem),
         scratch_shapes=[
@@ -383,7 +412,7 @@
             pltpu.VMEM((ITERS, points, rank), F32),
             pltpu.VMEM((ITERS, nz - 1, zrows, rank), F32),
             pltpu.VMEM((ITERS, points, rank), F32),
-            pltpu.VMEM((ITERS, 3, 8, 1, 128), F32),
+            pltpu.VMEM((3, 8, 1, ITERS * 128), F32),
             pltpu.VMEM((ITERS, NX * NY * NC, 1, 2 * rank), F32),
             pltpu.VMEM((ITERS, nz, 1, 2 * rank), F32),
             pltpu.SemaphoreType.DMA((6 + blocks,)),

time: 64.9 us -> 64.5 us (level)
  no operation moved by 1% of the time
where the time goes in v4:
time: 64.5 us; the launch traced here: 64.3 us
  Pallas kernels  63.7 us (99%)
    pallas_call x1, Pallas kernels, shards(): pl.pallas_call(functools.partial(kernel, nz), out_shape=outs[:2] + (jax.S...  62.3 us
    pallas_call x1, Pallas kernels, shards(): pl.pallas_call(store, out_shape=outs, in_specs=[vmem, vmem, vmem], out_sp...  1.41 us

profile of v4, /device:TPU:1, one launch (start us, length us, event | category | flops | bytes accessed | tf_op | source)
XLA Modules:
  0.0 64.3 jit_solution(1173338377362212946)
XLA Ops:
  0.6 62.3 %shard_map.94 = (f32[512,128]{1,0:T(8,128)S(1)}, f32[1024,128]{1,0:T(8,128)S(1)}, f32[1,256]{1,0:T(1,128)S(1)}) custom-call(f32[512,128]{1,0:T(8,128)} %s_in.1, f32[1024,128]{1,0:T(8,128)} %u_in.1, f32[512,1024]{1,0:T(8,128)} %sig_in.1, f32[4,128]{1,0:T(4,128)} %bitcast.2, f32[4,128]{1,0:T(4,128)} %bitcast.3, f32[128,128]{1,0:T(8,128)} %inv_s_in.1, ...), custom_call_target="tpu_custom_call" | custom-call | tf_op jit(solution)/shard_map/pallas_call | solution.py:382
  62.9 1.4 %shard_map.95 = (f32[512,128]{1,0:T(8,128)}, f32[1024,128]{1,0:T(8,128)}, f32[2]{0:T(128)}) custom-call(f32[512,128]{1,0:T(8,128)S(1)} %get-tuple-element.6.s, f32[1024,128]{1,0:T(8,128)S(1)} %get-tuple-element.7.u, f32[1,256]{1,0:T(1,128)S(1)} %get-tuple-element.8.mis), custom_call_target="tpu_custom_call" | custom-call | tf_op jit(solution)/shard_map/pallas_call | solution.py:427

commit v5 on v4

--- a/solution.py
+++ b/solution.py
@@ -30,7 +30,7 @@
 
 def kernel(nz, s_in, u_in, sig_in, rate_in, power_in, inv_s_in, inv_t_in, s_out, u_out, mis_out,
            s0, u0, sig, rate, power, inv_s, inv_t,
-           sig_lr, sig_ex, lr, ex, a_ref, at_ref, b_ref, rec, fh, fl, tp, cr, th, xr, ts, yr, u_nx, sp, zr, s_nx, nv, n_xy, n_z,
+           raw_fluid, raw_expo, fluid, ex, a_ref, at_ref, b_ref, rec, fh, fl, tp, cr, th, xr, ts, yr, u_nx, sp, zr, s_nx, nv, n_xy, n_z,
            load, send, recv):
     points, rank = s0.shape
     moments = u0.shape[0]
@@ -118,12 +118,12 @@
     power_load.wait()
     for k in range(points // 128):
         rows = pl.ds(k * 128, 128)
-        sig_lr[rows, :] = jnp.broadcast_to(jnp.log2(rate[k : k + 1, :]), (128, 128)).T
-        sig_ex[rows, :] = jnp.broadcast_to(0.5 * (power[k : k + 1, :] - 1.0), (128, 128)).T
+        raw_fluid[rows, :] = jnp.broadcast_to(rate[k : k + 1, :], (128, 128)).T
+        raw_expo[rows, :] = jnp.broadcast_to(0.5 * (power[k : k + 1, :] - 1.0), (128, 128)).T
     for r, q in enumerate(turned):
         rows = pl.ds(r * zrows, zrows)
-        lr[rows, :] = sig_lr[pl.ds(q, zrows), :]
-        ex[rows, :] = sig_ex[pl.ds(q, zrows), :]
+        fluid[rows, :] = raw_fluid[pl.ds(q, zrows), :]
+        ex[rows, :] = raw_expo[pl.ds(q, zrows), :]
     u_load.wait()
     sig_load += fetch_stress(range(2, blocks))
     inv_loads = [fetch(inv_s_in, inv_s), fetch(inv_t_in, inv_t)]
@@ -147,7 +147,7 @@
         def transpose_modes():
             for k in range(nz // 2):
                 rows = pl.ds(2 * k * zrows, 2 * zrows)
-                hi, lo = split(turned_modes(k).T)
+                hi, lo = split((turned_modes(k) * fluid[rows, :]).T)
                 at_ref[:rank, rows] = hi
                 at_ref[rank:, rows] = lo
 
@@ -165,7 +165,7 @@
                     stress = sig[k, pl.ds(q, zrows), :] - rec[m % 2, rows, pl.ds((k % 2) * xrows, xrows)]
                     quad = stress * stress
                     mis = mis + jnp.sum(quad.reshape(zrows // 8, 8, 128), axis=0)
-                    flow = stress * jnp.exp2(lr[rows, :] + ex[rows, :] * jnp.log2(quad + 1e-6))
+                    flow = stress * jnp.exp2(ex[rows, :] * jnp.log2(quad + 1e-6))
                     hi, lo = split(flow)
                     fh[rows, lanes] = hi
                     fl[rows, lanes] = lo
@@ -180,7 +180,7 @@
         def send_space(h):
             pts = pl.ds(h * (points // 2), points // 2)
             pair = dot(fh[pts, :], b_ref[:, rank : 3 * rank], 1, 0)
-            sp[it, pts, :] = pair[:, :rank] + pair[:, rank:] + dot(fl[pts, :], b_ref[:, :rank], 1, 0)
+            sp[it, pts, :] = fluid[pts, :] * (pair[:, :rank] + pair[:, rank:] + dot(fl[pts, :], b_ref[:, :rank], 1, 0))
             for r in range(h * nz // 2, min((h + 1) * nz // 2, nz - 1)):
                 put(sp.at[it, pl.ds(r * zrows, zrows), :], zr.at[it, r], it, Z_SUM, p, z_peers[r])
 

time: 64.5 us -> 64.6 us (level)
  no operation moved by 1% of the time
where the time goes in v5:
time: 64.6 us; the launch traced here: 64.4 us
  Pallas kernels  63.8 us (99%)
    pallas_call x1, Pallas kernels, shards(): pl.pallas_call(functools.partial(kernel, nz), out_shape=outs[:2] + (jax.S...  62.4 us
    pallas_call x1, Pallas kernels, shards(): pl.pallas_call(store, out_shape=outs, in_specs=[vmem, vmem, vmem], out_sp...  1.41 us

profile of v5, /device:TPU:1, one launch (start us, length us, event | category | flops | bytes accessed | tf_op | source)
XLA Modules:
  0.0 64.4 jit_solution(9100587910718576386)
XLA Ops:
  0.6 62.4 %shard_map.94 = (f32[512,128]{1,0:T(8,128)S(1)}, f32[1024,128]{1,0:T(8,128)S(1)}, f32[1,256]{1,0:T(1,128)S(1)}) custom-call(f32[512,128]{1,0:T(8,128)} %s_in.1, f32[1024,128]{1,0:T(8,128)} %u_in.1, f32[512,1024]{1,0:T(8,128)} %sig_in.1, f32[4,128]{1,0:T(4,128)} %bitcast.2, f32[4,128]{1,0:T(4,128)} %bitcast.3, f32[128,128]{1,0:T(8,128)} %inv_s_in.1, ...), custom_call_target="tpu_custom_call" | custom-call | tf_op jit(solution)/shard_map/pallas_call | solution.py:382
  63.0 1.4 %shard_map.95 = (f32[512,128]{1,0:T(8,128)}, f32[1024,128]{1,0:T(8,128)}, f32[2]{0:T(128)}) custom-call(f32[512,128]{1,0:T(8,128)S(1)} %get-tuple-element.6.s, f32[1024,128]{1,0:T(8,128)S(1)} %get-tuple-element.7.u, f32[1,256]{1,0:T(1,128)S(1)} %get-tuple-element.8.mis), custom_call_target="tpu_custom_call" | custom-call | tf_op jit(solution)/shard_map/pallas_call | solution.py:427
